TPU v7x, 256 devices: a whole 4x4x8 slice. The times are simulated.
256 devices in a mesh: dom: 64 (over z, y, core), bin: 4 (over x).
Axes of the slice: x: 4, y: 4, z: 8, core: 2. Of those that a mesh axis runs over, the one named last changes fastest.
Arguments:
- field_in: float32 [8, 1048576], P(None, ('dom', 'bin')), may hold values from -6 to 6
- heading_in: float32 [3, 1048576], P(None, ('dom', 'bin')), may hold values from -3 to 3
- launch_domain: int32 [1048576, 1], P(('dom', 'bin')), may hold values from 0 to 63; in each aligned block of 4096 rows (0 to 4095, 4096 to 8191, ...) at most 128 rows name the same one
- hop_domain: int32 [3, 1048576, 1], P(None, ('dom', 'bin')), may hold values from 0 to 63; in each aligned block of 4096 rows (0 to 4095, 4096 to 8191, ..., all dimensions but the last counted through in order) at most 128 rows name the same one
- hit_facet: int32 [4, 1048576], P(None, ('dom', 'bin')), may hold values from 0 to 8191
- path_phase: float32 [4, 1048576], P(None, ('dom', 'bin')), may hold values from -3.140625 to 3.140625
- facet_polar: float32 [524288], P('dom'), may hold values from -3.140625 to 3.140625
- facet_azimuth: float32 [524288], P('dom'), may hold values from -3.140625 to 3.140625
- facet_tilt: float32 [524288], P('dom'), may hold values from -3.140625 to 3.140625
- surface_resistance: float32 [524288], P('dom'), may hold values from 0.2 to 5
- surface_reactance: float32 [524288], P('dom'), may hold values from -1 to 1
- kernel: bfloat16 [2, 524288, 1024], P(None, ('dom', 'bin')), may hold values from -0.00390625 to 0.00390625
Outputs:
- far_field: float32 [8, 1024], P(None, ('dom', 'bin'))
- exit_field: float32 [8, 1048576], P(None, ('dom', 'bin'))
Inputs may be any that keep to these rules, and one draw needn't show every extreme that they name: `launch_domain`: among the 4096 tubes launched from one device (aligned blocks of the tube dimension), each domain is named at most 128 times in each bounce, and exactly 128 times by some domain in some blocks. `hop_domain`: among the 4096 tubes launched from one device, each domain is named at most 128 times in each bounce, and exactly 128 times by some domain in some blocks.
All inputs are finite; a program needn't handle non-finite values.
Results may differ from a plain program's by a relative error of at most 0.0029.
Values sent between devices are 32-bit elements; how exact they have to be, the bound alone decides.
A program may use at most 128 MiB of HBM per device.

v0:
```python
import jax
import jax.numpy as jnp
from jax import lax
from jax.sharding import PartitionSpec as P

BOUNCES = 4


def sent_together(arrays, axis, split_dim, concat_dim, along):
    both = jnp.concatenate(arrays, axis=along)
    whole, at, outs = (
        lax.all_to_all(both, axis, split_axis=split_dim, concat_axis=concat_dim, tiled=True),
        0,
        [],
    )
    for a in arrays:
        outs.append(lax.slice_in_dim(whole, at, at + a.shape[along], axis=along))
        at += a.shape[along]
    return tuple(outs)


def in_blocks(value, dim, count):
    lengths = value.shape
    blocks = value.reshape(*lengths[:dim], count, lengths[dim] // count, *lengths[dim + 1 :])
    return jnp.moveaxis(blocks, dim, 0)


def sent_and_summed(value, axis, dim):
    count = lax.axis_size(axis)
    blocks = lax.all_to_all(in_blocks(value, dim, count), axis, 0, 0, tiled=True)
    return jnp.sum(blocks, axis=0)


def facet_frame(polar_angle, azimuth, tilt_angle, resistance, reactance):
    return jnp.stack(
        [
            jnp.sin(polar_angle) * jnp.cos(azimuth),
            jnp.sin(polar_angle) * jnp.sin(azimuth),
            jnp.cos(polar_angle),
            resistance,
            reactance,
            jnp.cos(tilt_angle),
            jnp.sin(tilt_angle),
        ],
        axis=0,
    )


def divide(top_real, top_imag, low_real, low_imag):
    modulus = low_real * low_real + low_imag * low_imag
    return (
        (top_real * low_real + top_imag * low_imag) / modulus,
        (top_imag * low_real - top_real * low_imag) / modulus,
    )


def turn_phase(tube_field, phase_angle):
    phase_cos = jnp.cos(phase_angle)
    phase_sin = jnp.sin(phase_angle)
    return jnp.concatenate(
        [
            phase_cos * tube_field[0:4] - phase_sin * tube_field[4:8],
            phase_sin * tube_field[0:4] + phase_cos * tube_field[4:8],
        ],
        axis=0,
    )


def reflect(tube_field, heading, facet_rows):
    normal = facet_rows[0:3]
    incidence = jnp.sum(heading * normal, axis=0)
    cosine = jnp.abs(incidence)
    eta_real = facet_rows[3]
    eta_imag = facet_rows[4]
    tilt_cos = facet_rows[5]
    tilt_sin = facet_rows[6]
    te_real, te_imag = divide(cosine - eta_real, -eta_imag, cosine + eta_real, eta_imag)
    tm_real, tm_imag = divide(
        eta_real * cosine - 1.0, eta_imag * cosine, eta_real * cosine + 1.0, eta_imag * cosine
    )
    upper_real = tilt_cos * tube_field[0:2] + tilt_sin * tube_field[2:4]
    lower_real = tilt_cos * tube_field[2:4] - tilt_sin * tube_field[0:2]
    upper_imag = tilt_cos * tube_field[4:6] + tilt_sin * tube_field[6:8]
    lower_imag = tilt_cos * tube_field[6:8] - tilt_sin * tube_field[4:6]
    result = jnp.concatenate(
        [
            te_real * upper_real - te_imag * upper_imag,
            tm_real * lower_real - tm_imag * lower_imag,
            te_real * upper_imag + te_imag * upper_real,
            tm_real * lower_imag + tm_imag * lower_real,
        ],
        axis=0,
    )
    turned = heading - 2.0 * incidence * normal
    return (result, turned)


def slot_numbers(target, domains, capacity):
    tube_rows = target.shape[0]
    block_rows = min(512, tube_rows)
    markers = (target[:, None] == jnp.arange(domains, dtype=jnp.int32)[None, :]).astype(
        jnp.bfloat16
    )
    markers = markers.reshape(tube_rows // block_rows, block_rows, domains)
    lower_mask = (jnp.arange(block_rows)[:, None] >= jnp.arange(block_rows)[None, :]).astype(
        jnp.bfloat16
    )
    inside = jnp.einsum("ij,bjd->bid", lower_mask, markers, preferred_element_type=jnp.float32)
    totals = inside[:, -1, :]
    before = jnp.cumsum(totals, axis=0) - totals
    counts = inside + before[:, None, :]
    ranking = jnp.sum(counts * markers.astype(jnp.float32), axis=2).reshape(tube_rows) - 1.0
    return target * capacity + ranking.astype(jnp.int32)


def body(
    field_in,
    heading_in,
    launch_domain,
    hop_domain,
    hit_facet,
    path_phase,
    facet_polar,
    facet_azimuth,
    facet_tilt,
    surface_resistance,
    surface_reactance,
    kernel,
):
    domains = lax.axis_size("dom")
    tube_rows = field_in.shape[1]
    capacity = 2 * tube_rows // domains
    facet_count = facet_polar.shape[0]
    tube_field = field_in
    heading = heading_in
    frame_local = facet_frame(
        facet_polar, facet_azimuth, facet_tilt, surface_resistance, surface_reactance
    )
    facet_sums = jnp.zeros((8, facet_count), jnp.float32)
    for bounce in range(BOUNCES):
        if bounce == 0:
            target = launch_domain[:, 0]
        else:
            target = hop_domain[bounce - 1, :, 0]
        facet_ids = hit_facet[bounce]
        phased = turn_phase(tube_field, path_phase[bounce])
        slot_index = slot_numbers(target, domains, capacity)
        send_field = (
            jnp.zeros((8, domains * capacity), jnp.float32)
            .at[:, slot_index]
            .set(phased)
            .reshape(8, domains, capacity)
        )
        send_heading = (
            jnp.zeros((3, domains * capacity), jnp.float32)
            .at[:, slot_index]
            .set(heading)
            .reshape(3, domains, capacity)
        )
        send_ids = (
            jnp.zeros((domains * capacity,), jnp.int32)
            .at[slot_index]
            .set(facet_ids)
            .reshape(domains, capacity)
        )
        got_field, got_heading = sent_together((send_field, send_heading), "dom", 1, 1, 0)
        got_ids = lax.all_to_all(send_ids, "dom", split_axis=0, concat_axis=0, tiled=True).reshape(
            domains * capacity
        )
        facet_rows = jnp.take(frame_local, got_ids, axis=1)
        out_field, out_heading = reflect(
            got_field.reshape(8, domains * capacity),
            got_heading.reshape(3, domains * capacity),
            facet_rows,
        )
        facet_sums = facet_sums.at[:, got_ids].add(out_field)
        back_field, back_heading = sent_together(
            (out_field.reshape(8, domains, capacity), out_heading.reshape(3, domains, capacity)),
            "dom",
            1,
            1,
            0,
        )
        tube_field = back_field.reshape(8, domains * capacity)[:, slot_index]
        heading = back_heading.reshape(3, domains * capacity)[:, slot_index]
    quarter = sent_and_summed(facet_sums, "bin", 1)
    rounded = quarter.astype(jnp.bfloat16)
    real_part = jnp.dot(rounded, kernel[0], preferred_element_type=jnp.float32)
    imag_part = jnp.dot(rounded, kernel[1], preferred_element_type=jnp.float32)
    partial_value = jnp.concatenate(
        [real_part[0:4] - imag_part[4:8], imag_part[0:4] + real_part[4:8]], axis=0
    )
    far_field = lax.psum_scatter(partial_value, ("dom", "bin"), scatter_dimension=1, tiled=True)
    return (far_field, tube_field)


def solution(mesh):
    in_specs = (
        P(None, ("dom", "bin")),
        P(None, ("dom", "bin")),
        P(("dom", "bin"), None),
        P(None, ("dom", "bin"), None),
        P(None, ("dom", "bin")),
        P(None, ("dom", "bin")),
        P("dom"),
        P("dom"),
        P("dom"),
        P("dom"),
        P("dom"),
        P(None, ("dom", "bin"), None),
    )
    out_specs = (P(None, ("dom", "bin")), P(None, ("dom", "bin")))
    return jax.shard_map(body, mesh=mesh, in_specs=in_specs, out_specs=out_specs, check_vma=False)
```

profile of v0, /device:TPU:1, one launch (start us, length us, event | category | flops | bytes accessed | tf_op | source)
XLA Modules:
  0.0 1007.9 jit_solution(7003264734439389769)
XLA Ops:
  6.2 16.1 %scatter_custom_fusion.4 = s32[8192]{0:T(1024)} fusion(s32[4096]{0:T(1024)S(1)} %bitcast.603, s32[4096]{0:T(1024)S(1)} %bitcast.621, s32[]{:T(128)} %constant.36.clone.1), kind=kCustom, calls=%fused_computation.298 | custom fusion | bytes 32772 | tf_op jit(solution)/shard_map/scatter | solution.py:163
  22.3 13.1 %all-to-all-start.2 = ((s32[64,1,128]{2,1,0:T(1,128)}), s32[64,1,128]{2,1,0:T(1,128)S(1)}, u32[]{:S(2)}, u32[]{:S(2)}) async-start(s32[64,1,128]{2,1,0:T(1,128)} %bitcast.39), calls=%async_computation.2 | async-start | bytes 65536 | tf_op jit(solution)/shard_map/all_to_all | solution.py:167
  40.7 16.1 %scatter_custom_fusion.12 = s32[8192]{0:T(1024)} fusion(s32[4096]{0:T(1024)S(1)} %bitcast.596, s32[4096]{0:T(1024)S(1)} %bitcast.620, s32[]{:T(128)} %constant.36.clone.1), kind=kCustom, calls=%fused_computation.294 | custom fusion | bytes 32772 | tf_op jit(solution)/shard_map/scatter | solution.py:163
  56.8 16.1 %scatter_custom_fusion.8 = s32[8192]{0:T(1024)} fusion(s32[4096]{0:T(1024)S(1)} %bitcast.600, s32[4096]{0:T(1024)S(1)} %bitcast.619, s32[]{:T(128)} %constant.36.clone.1), kind=kCustom, calls=%fused_computation.296 | custom fusion | bytes 32772 | tf_op jit(solution)/shard_map/scatter | solution.py:163
  74.1 16.2 %scatter_custom_fusion = s32[8192]{0:T(1024)} fusion(s32[4096]{0:T(1024)S(1)} %bitcast.609, s32[4096]{0:T(1024)S(1)} %bitcast.618, s32[]{:T(128)} %constant.36.clone.1), kind=kCustom, calls=%fused_computation.300 | custom fusion | bytes 32772 | tf_op jit(solution)/shard_map/scatter | solution.py:163
  91.1 12.8 %scatter_custom_fusion.1 = f32[8,8192]{0,1:T(8,128)} fusion(s32[4096]{0:T(1024)S(1)} %bitcast.610, f32[4096,8]{1,0:T(8,128)S(1)} %copy.297, f32[]{:T(128)} %constant.18.clone.1), kind=kCustom, calls=%fused_computation.52 | custom fusion | bytes 262148 | tf_op jit(solution)/shard_map/scatter | solution.py:151
  107.3 12.8 %scatter_custom_fusion.2 = f32[3,8192]{0,1:T(8,128)} fusion(s32[4096]{0:T(1024)S(1)} %bitcast.611, f32[4096,3]{1,0:T(8,128)S(1)} %copy.298, f32[]{:T(128)} %constant.18.clone.1), kind=kCustom, calls=%fused_computation.42 | custom fusion | bytes 98308 | tf_op jit(solution)/shard_map/scatter | solution.py:157
  180.1 29.9 %gather_fusion.7 = f32[8192,7]{1,0:T(8,128)} fusion(f32[7,8192]{0,1:T(8,128)} %copy.301, s32[8192]{0:T(1024)S(1)} %fusion.81), kind=kCustom, calls=%fused_computation.3.clone | custom fusion | bytes 491520 | tf_op jit(solution)/shard_map/jit(_take)/gather | solution.py:170
  212.9 29.9 %gather_fusion.6 = f32[8192,7]{1,0:T(8,128)} fusion(f32[7,8192]{0,1:T(8,128)} %copy.301, s32[8192]{0:T(1024)S(1)} %fusion.80), kind=kCustom, calls=%fused_computation.2.clone | custom fusion | bytes 491520 | tf_op jit(solution)/shard_map/jit(_take)/gather | solution.py:170
  245.6 29.9 %gather_fusion.5 = f32[8192,7]{1,0:T(8,128)} fusion(f32[7,8192]{0,1:T(8,128)} %copy.301, s32[8192]{0:T(1024)S(1)} %fusion.79), kind=kCustom, calls=%fused_computation.1.clone | custom fusion | bytes 491520 | tf_op jit(solution)/shard_map/jit(_take)/gather | solution.py:170
  278.4 29.9 %gather_fusion.4 = f32[8192,7]{1,0:T(8,128)} fusion(f32[7,8192]{0,1:T(8,128)} %copy.301, s32[8192]{0:T(1024)S(1)} %fusion.78), kind=kCustom, calls=%fused_computation.clone | custom fusion | bytes 491520 | tf_op jit(solution)/shard_map/jit(_take)/gather | solution.py:170
  316.4 10.4 %all-to-all-start.3 = ((f32[11,64,128]{2,0,1:T(8,128)}), f32[11,64,128]{2,0,1:T(8,128)S(1)}, u32[]{:S(2)}, u32[]{:S(2)}) async-start(f32[11,64,128]{2,0,1:T(8,128)} %concatenate.62), calls=%async_computation.3 | async-start | bytes 1048576 | tf_op jit(solution)/shard_map/all_to_all | solution.py:12
  328.5 16.1 %all-to-all-done.3 = f32[11,64,128]{2,0,1:T(8,128)S(1)} async-done(((f32[11,64,128]{2,0,1:T(8,128)}), f32[11,64,128]{2,0,1:T(8,128)S(1)}, u32[]{:S(2)}, u32[]{:S(2)}) %all-to-all-start.3) | async-done | bytes 360480 | tf_op jit(solution)/shard_map/all_to_all | solution.py:12
  347.2 13.0 %gather_fusion = f32[4096,8]{1,0:T(8,128)S(1)} fusion(f32[8,8192]{0,1:T(8,128)} %bitcast.492, s32[4096]{0:T(1024)S(1)} %broadcast_clamp_fusion.3), kind=kCustom, calls=%fused_computation.4 | custom fusion | bytes 278528 | tf_op jit(solution)/shard_map/gather | solution.py:184
  362.1 12.9 %scatter_custom_fusion.5 = f32[8,8192]{0,1:T(8,128)} fusion(s32[4096]{0:T(1024)} %bitcast.605, f32[4096,8]{1,0:T(8,128)S(1)} %copy.307, f32[]{:T(128)} %constant.18.clone.1), kind=kCustom, calls=%fused_computation.48 | custom fusion | bytes 262656 | tf_op jit(solution)/shard_map/scatter | solution.py:151
  380.4 36.3 %scatter_custom_fusion.6 = f32[3,8192]{0,1:T(8,128)} fusion(s32[4096]{0:T(1024)} %bitcast.606, f32[3,8192]{0,1:T(8,128)} %bitcast.495, s32[4096]{0:T(1024)} %copy-done.11, f32[]{:T(128)} %constant.18.clone.1), kind=kCustom, calls=%fused_computation.37 | custom fusion | bytes 98816 | tf_op jit(solution)/shard_map/scatter | solution.py:157
  429.0 54.9 %scatter_custom_fusion.3 = f32[8,8192]{0,1:T(8,128)} fusion(s32[8192]{0:T(1024)} %bitcast.615, f32[8192,8]{1,0:T(8,128)} %copy.303, f32[]{:T(128)} %constant.18.clone.1), kind=kCustom, calls=%fused_computation.50 | custom fusion | flops 65536 | bytes 262656 | tf_op jit(solution)/shard_map/scatter-add | solution.py:176
  496.6 17.4 %all-to-all-done.6 = f32[11,64,128]{2,0,1:T(8,128)S(1)} async-done(((f32[11,64,128]{2,0,1:T(8,128)}), f32[11,64,128]{2,0,1:T(8,128)S(1)}, u32[]{:S(2)}, u32[]{:S(2)}) %all-to-all-start.6) | async-done | bytes 360480 | tf_op jit(solution)/shard_map/all_to_all | solution.py:12
  516.7 13.0 %gather_fusion.1 = f32[4096,8]{1,0:T(8,128)S(1)} fusion(f32[8,8192]{0,1:T(8,128)} %bitcast.493, s32[4096]{0:T(1024)S(1)} %copy-done.10), kind=kCustom, calls=%fused_computation.6 | custom fusion | bytes 278528 | tf_op jit(solution)/shard_map/gather | solution.py:184
  531.6 13.1 %scatter_custom_fusion.9 = f32[8,8192]{0,1:T(8,128)} fusion(s32[4096]{0:T(1024)} %bitcast.601, f32[4096,8]{1,0:T(8,128)S(1)} %copy.317, f32[]{:T(128)} %constant.18.clone.1), kind=kCustom, calls=%fused_computation.46 | custom fusion | bytes 262656 | tf_op jit(solution)/shard_map/scatter | solution.py:151
  550.2 35.9 %scatter_custom_fusion.10 = f32[3,8192]{0,1:T(8,128)} fusion(s32[4096]{0:T(1024)} %bitcast.602, f32[3,8192]{0,1:T(8,128)} %bitcast.496, s32[4096]{0:T(1024)} %broadcast_clamp_fusion.2, f32[]{:T(128)} %constant.18.clone.1), kind=kCustom, calls=%fused_computation.35 | custom fusion | bytes 98816 | tf_op jit(solution)/shard_map/scatter | solution.py:157
  598.3 47.4 %scatter_fusion = f32[8,8192]{0,1:T(8,128)} fusion(f32[8,8192]{0,1:T(8,128)} %scatter_custom_fusion.3, s32[8192]{0:T(1024)S(1)} %bitcast.576, f32[8192,8]{1,0:T(8,128)} %copy.313), kind=kCustom, calls=%fused_computation.18 | custom fusion | flops 65536 | bytes 819200 | tf_op jit(solution)/shard_map/scatter-add | solution.py:176
  648.3 18.7 %all-to-all-start.9 = ((f32[11,64,128]{2,0,1:T(8,128)}), f32[11,64,128]{2,0,1:T(8,128)S(1)}, u32[]{:S(2)}, u32[]{:S(2)}) async-start(f32[11,64,128]{2,0,1:T(8,128)} %concatenate.70), calls=%async_computation.9 | async-start | bytes 1048576 | tf_op jit(solution)/shard_map/all_to_all | solution.py:12
  667.4 17.2 %all-to-all-done.9 = f32[11,64,128]{2,0,1:T(8,128)S(1)} async-done(((f32[11,64,128]{2,0,1:T(8,128)}), f32[11,64,128]{2,0,1:T(8,128)S(1)}, u32[]{:S(2)}, u32[]{:S(2)}) %all-to-all-start.9) | async-done | bytes 360480 | tf_op jit(solution)/shard_map/all_to_all | solution.py:12
  687.2 13.0 %gather_fusion.2 = f32[4096,8]{1,0:T(8,128)S(1)} fusion(f32[8,8192]{0,1:T(8,128)} %bitcast.494, s32[4096]{0:T(1024)S(1)} %copy-done.9), kind=kCustom, calls=%fused_computation.8 | custom fusion | bytes 278528 | tf_op jit(solution)/shard_map/gather | solution.py:184
  701.4 12.9 %scatter_custom_fusion.13 = f32[8,8192]{0,1:T(8,128)} fusion(s32[4096]{0:T(1024)} %bitcast.597, f32[4096,8]{1,0:T(8,128)S(1)} %copy.327, f32[]{:T(128)} %constant.18.clone.1), kind=kCustom, calls=%fused_computation.44 | custom fusion | bytes 262656 | tf_op jit(solution)/shard_map/scatter | solution.py:151
  719.9 35.9 %scatter_custom_fusion.14 = f32[3,8192]{0,1:T(8,128)} fusion(s32[4096]{0:T(1024)} %bitcast.598, f32[3,8192]{0,1:T(8,128)} %bitcast.497, s32[4096]{0:T(1024)S(1)} %copy-done.9, f32[]{:T(128)} %constant.18.clone.1), kind=kCustom, calls=%fused_computation.33 | custom fusion | bytes 98816 | tf_op jit(solution)/shard_map/scatter | solution.py:157
  767.9 47.7 %scatter_fusion.1 = f32[8,8192]{0,1:T(8,128)} fusion(f32[8,8192]{0,1:T(8,128)} %scatter_fusion, s32[8192]{0:T(1024)S(1)} %bitcast.575, f32[8192,8]{1,0:T(8,128)} %copy.323), kind=kCustom, calls=%fused_computation.22 | custom fusion | flops 65536 | bytes 819200 | tf_op jit(solution)/shard_map/scatter-add | solution.py:176
  819.2 47.7 %scatter_fusion.2 = f32[8,8192]{0,1:T(8,128)} fusion(f32[8,8192]{0,1:T(8,128)} %scatter_fusion.1, s32[8192]{0:T(1024)S(1)} %bitcast.574, f32[8192,8]{1,0:T(8,128)} %copy.333), kind=kCustom, calls=%fused_computation.26 | custom fusion | flops 65536 | bytes 819200 | tf_op jit(solution)/shard_map/scatter-add | solution.py:176
  879.9 27.7 %all-to-all-start.12 = ((f32[11,64,128]{2,0,1:T(8,128)}), f32[11,64,128]{2,0,1:T(8,128)S(1)}, u32[]{:S(2)}, u32[]{:S(2)}) async-start(f32[11,64,128]{2,0,1:T(8,128)} %concatenate.75), calls=%async_computation.12 | async-start | bytes 1048576 | tf_op jit(solution)/shard_map/all_to_all | solution.py:12
  913.6 76.3 %all-reduce = f32[8,1024]{1,0:T(8,128)S(1)} all-reduce(f32[8,1024]{1,0:T(8,128)S(1)} %pad_maximum_fusion.4), channel_id=2, replica_groups=mesh['dom'=64,'bin'=4] {'dom','bin'}, use_global_device_ids=true, to_apply=%region_29.31.clone | all-reduce | flops 8192 | bytes 65536
  993.3 13.0 %gather_fusion.3 = f32[4096,8]{1,0:T(8,128)S(1)} fusion(f32[8,8192]{0,1:T(8,128)} %bitcast.491, s32[4096]{0:T(1024)S(1)} %broadcast_clamp_fusion), kind=kCustom, calls=%fused_computation.10 | custom fusion | bytes 278528 | tf_op jit(solution)/shard_map/gather | solution.py:184
  (225 shorter events, 202.6 us)
Async XLA Ops:
  2.6 34.0 %copy-start.16 = (s32[4096,1]{0,1:T(1,128)S(1)}, s32[4096,1]{0,1:T(1,128)}, u32[]{:S(2)}) copy-start(s32[4096,1]{0,1:T(1,128)} %param.16) | copy-start | bytes 49156
  2.6 34.7 %copy-start.20 = (f32[8192]{0:T(1024)S(1)}, f32[8192]{0:T(1024)}, u32[]{:S(2)}) copy-start(f32[8192]{0:T(1024)} %param.20) | copy-start | bytes 98308
  3.1 34.3 %copy-start.21 = (f32[8192]{0:T(1024)S(1)}, f32[8192]{0:T(1024)}, u32[]{:S(2)}) copy-start(f32[8192]{0:T(1024)} %param.22) | copy-start | bytes 98308
  3.1 34.4 %copy-start.12 = (f32[4,4096]{1,0:T(4,128)S(1)}, f32[4,4096]{1,0:T(4,128)}, u32[]{:S(2)}) copy-start(f32[4,4096]{1,0:T(4,128)} %param.19) | copy-start | bytes 196612
  4.3 86.1 %copy-start.8 = (f32[8,4096]{1,0:T(8,128)S(1)}, f32[8,4096]{1,0:T(8,128)}, u32[]{:S(2)}) copy-start(f32[8,4096]{1,0:T(8,128)} %param.14) | copy-start | bytes 393220
  6.2 31.1 %copy-start.19 = (s32[4096,1]{0,1:T(1,128)}, s32[4096,1]{0,1:T(1,128)S(1)}, u32[]{:S(2)}) copy-start(s32[4096,1]{0,1:T(1,128)S(1)} %get-tuple-element.99) | copy-start | bytes 49156
  6.2 84.3 %copy-start.17 = (s32[4096,1]{0,1:T(1,128)}, s32[4096,1]{0,1:T(1,128)S(1)}, u32[]{:S(2)}) copy-start(s32[4096,1]{0,1:T(1,128)S(1)} %get-tuple-element.98) | copy-start | bytes 49156
  6.2 97.6 %copy-start.18 = (s32[4096,1]{0,1:T(1,128)}, s32[4096,1]{0,1:T(1,128)S(1)}, u32[]{:S(2)}) copy-start(s32[4096,1]{0,1:T(1,128)S(1)} %get-tuple-element.100) | copy-start | bytes 49156
  22.3 104.6 %all-to-all-start.2 = ((s32[64,1,128]{2,1,0:T(1,128)}), s32[64,1,128]{2,1,0:T(1,128)S(1)}, u32[]{:S(2)}, u32[]{:S(2)}) async-start(s32[64,1,128]{2,1,0:T(1,128)} %bitcast.39), calls=%async_computation.2 | async-start | bytes 65536 | tf_op jit(solution)/shard_map/all_to_all | solution.py:167
  74.1 273.1 %copy-start.11 = (s32[4096]{0:T(1024)}, s32[4096]{0:T(1024)S(1)}, u32[]{:S(2)}) copy-start(s32[4096]{0:T(1024)S(1)} %broadcast_clamp_fusion.3) | copy-start | bytes 49156
  91.1 15.6 %copy-start.13 = (f32[3,4096]{1,0:T(4,128)S(1)}, f32[3,4096]{1,0:T(4,128)}, u32[]{:S(2)}) copy-start(f32[3,4096]{1,0:T(4,128)} %param.15) | copy-start | bytes 147460
  107.3 15.6 %copy-start.22 = (f32[8192]{0:T(1024)S(1)}, f32[8192]{0:T(1024)}, u32[]{:S(2)}) copy-start(f32[8192]{0:T(1024)} %param.21) | copy-start | bytes 98308
  107.3 15.8 %copy-start.23 = (f32[8192]{0:T(1024)S(1)}, f32[8192]{0:T(1024)}, u32[]{:S(2)}) copy-start(f32[8192]{0:T(1024)} %param.23) | copy-start | bytes 98308
  107.3 15.8 %copy-start.24 = (f32[8192]{0:T(1024)S(1)}, f32[8192]{0:T(1024)}, u32[]{:S(2)}) copy-start(f32[8192]{0:T(1024)} %param.24) | copy-start | bytes 98308
  126.9 19.7 %all-to-all-start.8 = ((s32[64,1,128]{2,1,0:T(1,128)}), s32[64,1,128]{2,1,0:T(1,128)S(1)}, u32[]{:S(2)}, u32[]{:S(2)}) async-start(s32[64,1,128]{2,1,0:T(1,128)} %bitcast.113), calls=%async_computation.8 | async-start | bytes 65536 | tf_op jit(solution)/shard_map/all_to_all | solution.py:167
  146.6 14.2 %all-to-all-start.5 = ((s32[64,1,128]{2,1,0:T(1,128)}), s32[64,1,128]{2,1,0:T(1,128)S(1)}, u32[]{:S(2)}, u32[]{:S(2)}) async-start(s32[64,1,128]{2,1,0:T(1,128)} %bitcast.76), calls=%async_computation.5 | async-start | bytes 65536 | tf_op jit(solution)/shard_map/all_to_all | solution.py:167
  160.9 14.1 %all-to-all-start = ((s32[64,1,128]{2,1,0:T(1,128)}), s32[64,1,128]{2,1,0:T(1,128)S(1)}, u32[]{:S(2)}, u32[]{:S(2)}) async-start(s32[64,1,128]{2,1,0:T(1,128)} %bitcast.4), calls=%async_computation | async-start | bytes 65536 | tf_op jit(solution)/shard_map/all_to_all | solution.py:167
  175.0 138.9 %all-to-all-start.1 = ((f32[11,64,128]{2,0,1:T(8,128)}), f32[11,64,128]{2,0,1:T(8,128)S(1)}, u32[]{:S(2)}, u32[]{:S(2)}) async-start(f32[11,64,128]{2,0,1:T(8,128)} %pad_maximum_fusion), calls=%async_computation.1 | async-start | bytes 1048576 | tf_op jit(solution)/shard_map/all_to_all | solution.py:12
  316.4 28.1 %all-to-all-start.3 = ((f32[11,64,128]{2,0,1:T(8,128)}), f32[11,64,128]{2,0,1:T(8,128)S(1)}, u32[]{:S(2)}, u32[]{:S(2)}) async-start(f32[11,64,128]{2,0,1:T(8,128)} %concatenate.62), calls=%async_computation.3 | async-start | bytes 1048576 | tf_op jit(solution)/shard_map/all_to_all | solution.py:12
  416.7 9.6 copy-start
  416.7 9.6 copy-start.1
  420.5 63.4 %all-to-all-start.4 = ((f32[11,64,128]{2,0,1:T(8,128)}), f32[11,64,128]{2,0,1:T(8,128)S(1)}, u32[]{:S(2)}, u32[]{:S(2)}) async-start(f32[11,64,128]{2,0,1:T(8,128)} %pad_maximum_fusion.1), calls=%async_computation.4 | async-start | bytes 1048576 | tf_op jit(solution)/shard_map/all_to_all | solution.py:12
  484.6 32.0 %copy-start.10 = (s32[4096]{0:T(1024)S(1)}, s32[4096]{0:T(1024)}, u32[]{:S(2)}) copy-start(s32[4096]{0:T(1024)} %broadcast_clamp_fusion.2) | copy-start | bytes 49156
  486.5 27.5 %all-to-all-start.6 = ((f32[11,64,128]{2,0,1:T(8,128)}), f32[11,64,128]{2,0,1:T(8,128)S(1)}, u32[]{:S(2)}, u32[]{:S(2)}) async-start(f32[11,64,128]{2,0,1:T(8,128)} %concatenate.66), calls=%async_computation.6 | async-start | bytes 1048576 | tf_op jit(solution)/shard_map/all_to_all | solution.py:12
  589.8 55.9 %all-to-all-start.7 = ((f32[11,64,128]{2,0,1:T(8,128)}), f32[11,64,128]{2,0,1:T(8,128)S(1)}, u32[]{:S(2)}, u32[]{:S(2)}) async-start(f32[11,64,128]{2,0,1:T(8,128)} %pad_maximum_fusion.2), calls=%async_computation.7 | async-start | bytes 1048576 | tf_op jit(solution)/shard_map/all_to_all | solution.py:12
  646.4 40.8 %copy-start.9 = (s32[4096]{0:T(1024)S(1)}, s32[4096]{0:T(1024)}, u32[]{:S(2)}) copy-start(s32[4096]{0:T(1024)} %broadcast_clamp_fusion.1) | copy-start | bytes 49156
  648.3 36.3 %all-to-all-start.9 = ((f32[11,64,128]{2,0,1:T(8,128)}), f32[11,64,128]{2,0,1:T(8,128)S(1)}, u32[]{:S(2)}, u32[]{:S(2)}) async-start(f32[11,64,128]{2,0,1:T(8,128)} %concatenate.70), calls=%async_computation.9 | async-start | bytes 1048576 | tf_op jit(solution)/shard_map/all_to_all | solution.py:12
  667.3 33.4 %copy-start.14 = (f32[1,4096]{1,0:T(1,128)S(1)}, f32[1,4096]{1,0:T(1,128)}, u32[]{:S(2)}) copy-start(f32[1,4096]{1,0:T(1,128)} %get-tuple-element.84) | copy-start | bytes 49156
  667.4 33.4 %copy-start.15 = (f32[1,4096]{1,0:T(1,128)S(1)}, f32[1,4096]{1,0:T(1,128)}, u32[]{:S(2)}) copy-start(f32[1,4096]{1,0:T(1,128)} %get-tuple-element.88) | copy-start | bytes 49156
  759.5 56.2 %all-to-all-start.10 = ((f32[11,64,128]{2,0,1:T(8,128)}), f32[11,64,128]{2,0,1:T(8,128)S(1)}, u32[]{:S(2)}, u32[]{:S(2)}) async-start(f32[11,64,128]{2,0,1:T(8,128)} %pad_maximum_fusion.3), calls=%async_computation.10 | async-start | bytes 1048576 | tf_op jit(solution)/shard_map/all_to_all | solution.py:12
  870.3 9.6 all-to-all-start.11
  879.9 110.8 %all-to-all-start.12 = ((f32[11,64,128]{2,0,1:T(8,128)}), f32[11,64,128]{2,0,1:T(8,128)S(1)}, u32[]{:S(2)}, u32[]{:S(2)}) async-start(f32[11,64,128]{2,0,1:T(8,128)} %concatenate.75), calls=%async_computation.12 | async-start | bytes 1048576 | tf_op jit(solution)/shard_map/all_to_all | solution.py:12
  (6 other events, 44.9 us)
where the time goes:
time: 1020 us; the launch traced here: 1010 us
  local copies, waits for them, and re-layouts  497 us (49%)
  other arithmetic  217 us (21%)
  starting transfers between devices  126 us (12%)
  waiting for transfers between devices  82.4 us (8%)
  blocking collectives  76.3 us (7%)
    scatter-add x4, other arithmetic, body(): facet_sums = facet_sums.at[:, got_ids].add(out_field)  198 us
    gather x8, local copies, waits for them, and re-layouts, body(): facet_rows = jnp.take(frame_local, got_ids, axis=1)  131 us
    scatter x4, local copies, waits for them, and re-layouts, body(): send_heading = jnp.zeros((3, domains * capacity), jnp.float32).at[:, slot...  121 us
    all_to_all x8, starting transfers between devices, sent_together(): lax.all_to_all(both, axis, split_axis=split_dim, concat_axis=concat_dim,...  88.8 us
    unnamed x1, blocking collectives  76.3 us
    scatter x4, local copies, waits for them, and re-layouts, body(): send_ids = jnp.zeros((domains * capacity,), jnp.int32).at[slot_index].set...  64.5 us
    gather x7, local copies, waits for them, and re-layouts, body(): tube_field = back_field.reshape(8, domains * capacity)[:, slot_index]  53.5 us
    scatter x4, local copies, waits for them, and re-layouts, body(): send_field = jnp.zeros((8, domains * capacity), jnp.float32).at[:, slot_i...  51.6 us
  transfers between devices with their start and end apart: 13, of which 7 were waited for; matrix products, arithmetic and copies ran while one was open for 39% of the time, Pallas kernels for 0%

commit v1 on v0

v1 whole, which is shorter than its diff:
```python
import jax
import jax.numpy as jnp
from jax import lax
from jax.experimental import pallas as pl
from jax.experimental.pallas import tpu as pltpu
from jax.sharding import PartitionSpec as P

BOUNCES = 4
HALVES = 2
EACH = BOUNCES // HALVES
DOMS = 64
BINS = 4
CAP = 128
LANES = 128
ROWS = 32
PARAMS = 5
BATCH = 16
F32 = jnp.float32
BF16 = jnp.bfloat16
I32 = jnp.int32
MESH = pl.DeviceIdType.MESH
LAST = (((1,), (1,)), ((), ()))


def iota(shape, dim):
    return lax.broadcasted_iota(I32, shape, dim)


def narrow(x):
    return x.astype(F32).astype(BF16)


def split(x):
    big = x.astype(BF16)
    return big, (x - big.astype(F32)).astype(BF16)


def one_hot(rows, depth):
    count = narrow(iota((depth, LANES), 0))
    one, zero = jnp.ones((depth, LANES), BF16), jnp.zeros((depth, LANES), BF16)
    hot = [jnp.where(count == narrow(jnp.broadcast_to(r, (depth, LANES))), one, zero) for r in rows]
    return jnp.concatenate(hot, axis=1)


def sin_cos(x):
    turns = jnp.floor(x * 0.6366197723675814 + 0.5)
    r = x - turns * 1.5703125
    r = r - turns * 4.83826794896e-4
    z = r * r
    s = ((-1.9515295891e-4 * z + 8.3321608736e-3) * z - 1.6666654611e-1) * z * r + r
    c = ((2.443315711809948e-5 * z - 1.388731625493765e-3) * z + 4.166664568298827e-2) * z * z
    c = c - 0.5 * z + 1.0
    odd = jnp.abs(turns) == 1.0
    near = turns == 0.0
    sine = jnp.where(odd, turns * c, jnp.where(near, s, -s))
    cosine = jnp.where(odd, -turns * s, jnp.where(near, c, -c))
    return sine, cosine


def divide(top_real, top_imag, low_real, low_imag):
    scale = 1.0 / (low_real * low_real + low_imag * low_imag)
    return (
        (top_real * low_real + top_imag * low_imag) * scale,
        (top_imag * low_real - top_real * low_imag) * scale,
    )


def lookup(table, rows, store):
    size = 32 * PARAMS
    found = jnp.dot(table[...], one_hot([r & 255 for r in rows], 256), preferred_element_type=F32)
    found = found[:size] + found[size:]
    for i, r in enumerate(rows):
        hi = jnp.broadcast_to(r >> 8, (8, LANES))
        group, line = hi >> 3, hi & 7
        for p in range(PARAMS):
            f = [
                found[32 * p + 8 * q : 32 * p + 8 * q + 8, LANES * i : LANES * (i + 1)]
                for q in range(4)
            ]
            y = jnp.where(
                group < 2, jnp.where(group == 0, f[0], f[1]), jnp.where(group == 2, f[2], f[3])
            )
            y = jnp.take_along_axis(y, line, axis=0, mode="promise_in_bounds")
            store(i, p, y[0:1])


def gathered_sums(rows, tiles):
    half = iota((16, LANES), 0) >> 3
    zero = jnp.zeros((16, LANES), BF16)
    parts = ([], [])
    for r, f in zip(rows, tiles):
        big = f.astype(BF16).astype(F32)
        hi = narrow(jnp.broadcast_to(r >> 8, (16, LANES)) - half)
        masks = [hi == jnp.asarray(2 * k, BF16) for k in range(16)]
        for part, value in zip(parts, (big, f - big)):
            twice = jnp.concatenate([value, value], axis=0).astype(BF16)
            part.append(jnp.concatenate([jnp.where(m, twice, zero) for m in masks], axis=0))
    left = jnp.concatenate([jnp.concatenate(part, axis=1) for part in parts], axis=0)
    total = lax.dot_general(
        left, one_hot([r & 255 for r in rows], 256), LAST, preferred_element_type=F32
    )
    return total[:256] + total[256:]


def ranks(b, target, facet, ids_out, slots):
    block = 2 * LANES
    blocks = ROWS // 2
    after = iota((block, 2 * block), 0) <= iota((block, 2 * block), 1)
    after = jnp.where(after | (iota((block, 2 * block), 1) >= block), 1.0, 0.0).astype(BF16)
    carry = jnp.zeros((DOMS, block), F32)
    doms = [target[b, n : n + 1, :] for n in range(ROWS)]
    marks = [one_hot(doms[2 * j : 2 * j + 2], DOMS) for j in range(blocks)]
    counts = jnp.dot(jnp.concatenate(marks, axis=0), after, preferred_element_type=F32)
    zero = jnp.zeros((DOMS, block), BF16)
    left, places = [], []
    for j in range(blocks):
        count = counts[DOMS * j : DOMS * (j + 1)]
        place = marks[j].astype(F32) * (count[:, :block] + carry)
        place = jnp.sum(place, axis=0, keepdims=True).astype(I32) - 1
        carry = carry + count[:, block:]
        for w in range(2):
            n = 2 * j + w
            mine = place[:, LANES * w : LANES * (w + 1)]
            slots[b, n : n + 1, :] = doms[n] * CAP + mine
            places.append(mine)
        ids = jnp.concatenate([facet[b, 2 * j + w : 2 * j + w + 1, :] for w in range(2)], axis=1)
        left.append(
            jnp.concatenate(
                [
                    jnp.where(marks[j] > zero, narrow(jnp.broadcast_to(v, (DOMS, block))), zero)
                    for v in (ids >> 7, ids & 127)
                ],
                axis=0,
            )
        )
    packed = lax.dot_general(
        jnp.concatenate(left, axis=1), one_hot(places, CAP), LAST, preferred_element_type=F32
    ).astype(I32)
    ids_out[:, b, :] = packed[:DOMS] * 128 + packed[DOMS:]


def reflection(b, frame, phase, heading, coef):
    polar, azimuth, tilt, res, rea = (frame[p] for p in range(PARAMS))
    sin_p, cos_p = sin_cos(polar)
    sin_a, cos_a = sin_cos(azimuth)
    sin_t, cos_t = sin_cos(tilt)
    sin_f, cos_f = sin_cos(phase[b])
    normal = (sin_p * cos_a, sin_p * sin_a, cos_p)
    d = [heading[k] for k in range(3)]
    m = d[0] * normal[0] + d[1] * normal[1] + d[2] * normal[2]
    cosine = jnp.abs(m)
    te_r, te_i = divide(cosine - res, -rea, cosine + res, rea)
    rc, xc = res * cosine, rea * cosine
    tm_r, tm_i = divide(rc - 1.0, xc, rc + 1.0, xc)
    coef[0] = cos_t
    coef[1] = sin_t
    coef[2] = te_r * cos_f - te_i * sin_f
    coef[3] = te_r * sin_f + te_i * cos_f
    coef[4] = tm_r * cos_f - tm_i * sin_f
    coef[5] = tm_r * sin_f + tm_i * cos_f
    for k in range(3):
        heading[k] = d[k] - 2.0 * m * normal[k]


def reflect(coef, field):
    row = iota((8, LANES), 0)
    is_upper = (row & 2) == 0
    is_real = row < 4
    for n in range(ROWS):
        cos_t, sin_t, te_r, te_i, tm_r, tm_i = (
            jnp.broadcast_to(coef[k, n : n + 1, :], (8, LANES)) for k in range(6)
        )
        f = field[n]
        other = jnp.where(is_upper, pltpu.roll(f, 6, 0), -pltpu.roll(f, 2, 0))
        q = cos_t * f + sin_t * other
        turned = pltpu.roll(q, 4, 0)
        turned = jnp.where(is_real, -turned, turned)
        field[n] = jnp.where(is_upper, te_r, tm_r) * q + jnp.where(is_upper, te_i, tm_i) * turned


def main_kernel(
    target, facet, table, phase, heading_in, field_in, weights,
    far, exit_field,
    held, weight_sem,
    ids_send, ids_got, slots, rows_table,
    facts_send, facts_got, frame, heading, coef, field,
    fields_send, fields_got, sums, sums_got, partial, along_got, piece, last_got,
    ids_sems, facts_ssem, facts_rsem, fields_ssem, fields_rsem, sums_sems, along_sems, last_sems,
):
    me, my_bin = lax.axis_index("dom"), lax.axis_index("bin")
    z, y, core = me // 8, (me // 2) % 4, me % 2

    def partner(k):
        return ((z + k // 8) % 8) * 8 + ((y + (k // 2) % 4) % 4) * 2 + (core + k % 2) % 2

    def same_z(k):
        dom = z * 8 + ((y + (k // 2) % 4) % 4) * 2 + (core + k % 2) % 2
        return dom, (my_bin + k // 8) % BINS

    def send(source, landing, ssem, rsem, dom, bin_at):
        pltpu.make_async_remote_copy(
            src_ref=source, dst_ref=landing, send_sem=ssem, recv_sem=rsem,
            device_id=(dom, bin_at), device_id_type=MESH,
        ).start()

    def await_bytes(ref, sem):
        pltpu.make_async_copy(ref, ref, sem).wait()

    fetch = pltpu.make_async_copy(weights, held, weight_sem)
    fetch.start()
    barrier = pltpu.get_barrier_semaphore()

    @pl.loop(1, DOMS)
    def _(k):
        pl.semaphore_signal(barrier, inc=1, device_id=(partner(k), my_bin), device_id_type=MESH)

    @pl.loop(8, 32)
    def _(k):
        pl.semaphore_signal(barrier, inc=1, device_id=same_z(k), device_id_type=MESH)

    @pl.loop(0, BOUNCES)
    def _(b):
        ranks(b, target, facet, ids_send, slots)

    for k in range(3):
        heading[k] = heading_in[k]
    for n in range(ROWS):
        field[n] = field_in[:, n * LANES : (n + 1) * LANES]
    big, small = split(table[...])
    rows_table[: 32 * PARAMS] = big
    rows_table[32 * PARAMS :] = small

    pl.semaphore_wait(barrier, DOMS - 1 + 24)

    @pl.loop(1, DOMS)
    def _(k):
        dom = partner(k)
        send(ids_send.at[dom], ids_got.at[me], ids_sems.at[0], ids_sems.at[1], dom, my_bin)

    ids_got[me] = ids_send[me]
    await_bytes(ids_send.at[pl.ds(0, DOMS - 1)], ids_sems.at[1])

    senders = BATCH // EACH

    @pl.loop(0, HALVES)
    def _(h):
        @pl.loop(0, DOMS // senders)
        def _(g):
            doms = [partner(g * senders + i) for i in range(senders)]
            asked = [ids_got[dom, pl.ds(EACH * h + w, 1), :] for dom in doms for w in range(EACH)]

            def store(i, p, value):
                facts_send[h, doms[i // EACH], p, i % EACH : i % EACH + 1, :] = value

            lookup(rows_table, asked, store)
            for i in range(senders):

                @pl.when(g * senders + i > 0)
                def _():
                    send(
                        facts_send.at[h, doms[i]], facts_got.at[h, me],
                        facts_ssem.at[h], facts_rsem.at[h], doms[i], my_bin,
                    )

        facts_got[h, me] = facts_send[h, me]

    @pl.loop(0, BOUNCES)
    def _(b):
        h, w = b // EACH, b % EACH

        @pl.when(w == 0)
        def _():
            await_bytes(facts_send.at[h, pl.ds(0, DOMS - 1)], facts_rsem.at[h])

        for p in range(PARAMS):
            rows = [
                facts_got[h, pl.ds(j, 32, stride=2), p, pl.ds(w, 1), :].reshape(32, LANES)
                for j in range(2)
            ]
            big, small = split(jnp.concatenate(rows, axis=1))
            rows_table[32 * p : 32 * (p + 1)] = big
            rows_table[32 * (PARAMS + p) : 32 * (PARAMS + p + 1)] = small
        for part in range(ROWS // BATCH):

            def store(i, p, value, part=part):
                frame[p, part * BATCH + i : part * BATCH + i + 1, :] = value

            lookup(
                rows_table,
                [slots[b, n : n + 1, :] for n in range(part * BATCH, (part + 1) * BATCH)],
                store,
            )
        reflection(b, frame, phase, heading, coef)
        reflect(coef, field)
        total = None
        for part in range(ROWS // BATCH):
            lines = range(part * BATCH, (part + 1) * BATCH)
            more = gathered_sums([slots[b, n : n + 1, :] for n in lines], [field[n] for n in lines])
            total = more if total is None else total + more
        for hi in range(32):
            fields_send[2 * hi, b] = total[8 * hi : 8 * hi + 8, :LANES]
            fields_send[2 * hi + 1, b] = total[8 * hi : 8 * hi + 8, LANES:]

        @pl.loop(1, DOMS)
        def _(k):
            dom = partner(k)
            send(
                fields_send.at[dom, b], fields_got.at[b, me],
                fields_ssem.at[b], fields_rsem.at[b], dom, my_bin,
            )

        fields_got[b, me] = fields_send[me, b]

    for n in range(ROWS):
        exit_field[:, n * LANES : (n + 1) * LANES] = field[n]

    sums[...] = jnp.zeros_like(sums)

    @pl.loop(0, BOUNCES)
    def _(b):
        await_bytes(fields_got.at[b, pl.ds(0, DOMS - 1)], fields_rsem.at[b])

        @pl.loop(0, DOMS // BATCH)
        def _(g):
            rows = [ids_got[g * BATCH + i, pl.ds(b, 1), :] for i in range(BATCH)]
            sums[...] += gathered_sums(rows, [fields_got[b, g * BATCH + i] for i in range(BATCH)])

    for k in range(1, BINS):
        other = (my_bin + k) % BINS
        send(
            sums.at[pl.ds(pl.multiple_of(other * 64, 64), 64)], sums_got.at[k - 1],
            sums_sems.at[0, k - 1], sums_sems.at[1, k - 1], me, other,
        )
    mine = sums[pl.ds(pl.multiple_of(my_bin * 64, 64), 64), :]
    fetch.wait()
    for k in range(1, BINS):
        await_bytes(sums_got.at[k - 1], sums_sems.at[1, k - 1])
        mine = mine + sums_got[k - 1]
    mine = mine.astype(BF16)

    width = 512
    is_real = iota((8, width), 0) < 4
    for at in range(0, 1024, width):
        real, imag = jnp.zeros((8, width), F32), jnp.zeros((8, width), F32)
        for hi in range(8):
            left = mine[8 * hi : 8 * hi + 8]
            lines = slice(256 * hi, 256 * (hi + 1))
            real = real + jnp.dot(left, held[0, lines, at : at + width], preferred_element_type=F32)
            imag = imag + jnp.dot(left, held[1, lines, at : at + width], preferred_element_type=F32)
        turned = pltpu.roll(imag, 4, 0)
        value = real + jnp.where(is_real, -turned, turned)
        for q in range(width // LANES):
            partial[at // LANES + q] = value[:, LANES * q : LANES * (q + 1)]

    @pl.loop(1, 8)
    def _(k):
        to = (z + k) % 8
        send(
            partial.at[to], along_got.at[z], along_sems.at[0], along_sems.at[1],
            to * 8 + me % 8, my_bin,
        )

    along_got[z] = partial[z]
    await_bytes(partial.at[pl.ds(0, 7)], along_sems.at[1])
    tile = along_got[0]
    for k in range(1, 8):
        tile = tile + along_got[k]
    piece[...] = tile
    spot = (me % 8) * BINS + my_bin

    @pl.loop(1, 32)
    def _(k):
        dom, bin_at = same_z(k)
        send(piece, last_got.at[spot], last_sems.at[0], last_sems.at[1], dom, bin_at)

    last_got[spot] = tile
    await_bytes(last_got.at[pl.ds(0, 31)], last_sems.at[1])
    tile = last_got[0]
    for k in range(1, 32):
        tile = tile + last_got[k]
    far[...] = tile

    await_bytes(ids_send.at[pl.ds(0, DOMS - 1)], ids_sems.at[0])
    for h in range(HALVES):
        await_bytes(facts_send.at[h, pl.ds(0, DOMS - 1)], facts_ssem.at[h])
    for b in range(BOUNCES):
        await_bytes(fields_got.at[b, pl.ds(0, DOMS - 1)], fields_ssem.at[b])
    for k in range(1, BINS):
        await_bytes(sums_got.at[k - 1], sums_sems.at[0, k - 1])
    await_bytes(partial.at[pl.ds(0, 7)], along_sems.at[0])
    await_bytes(last_got.at[pl.ds(0, 31)], last_sems.at[0])


def main(target, facet, table, phase, heading, field, weights):
    vmem = pltpu.VMEM
    dma = pltpu.SemaphoreType.DMA
    whole = pl.BlockSpec(memory_space=pltpu.VMEM)
    return pl.pallas_call(
        main_kernel,
        out_shape=(
            jax.ShapeDtypeStruct((8, LANES), F32),
            jax.ShapeDtypeStruct((8, ROWS * LANES), F32),
        ),
        in_specs=[whole] * 6 + [pl.BlockSpec(memory_space=pl.ANY)],
        out_specs=(whole, whole),
        scratch_shapes=[
            vmem((2, 2048, 1024), BF16),
            dma,
            vmem((DOMS, BOUNCES, CAP), I32),
            vmem((DOMS, BOUNCES, CAP), I32),
            vmem((BOUNCES, ROWS, LANES), I32),
            vmem((2 * 32 * PARAMS, 256), BF16),
            vmem((HALVES, DOMS, PARAMS, EACH, CAP), F32),
            vmem((HALVES, DOMS, PARAMS, EACH, CAP), F32),
            vmem((PARAMS, ROWS, LANES), F32),
            vmem((3, ROWS, LANES), F32),
            vmem((6, ROWS, LANES), F32),
            vmem((ROWS, 8, LANES), F32),
            vmem((DOMS, BOUNCES, 8, CAP), F32),
            vmem((BOUNCES, DOMS, 8, CAP), F32),
            vmem((256, 256), F32),
            vmem((BINS - 1, 64, 256), F32),
            vmem((8, 8, LANES), F32),
            vmem((8, 8, LANES), F32),
            vmem((8, LANES), F32),
            vmem((32, 8, LANES), F32),
            dma((2,)),
            dma((HALVES,)),
            dma((HALVES,)),
            dma((BOUNCES,)),
            dma((BOUNCES,)),
            dma((2, BINS - 1)),
            dma((2,)),
            dma((2,)),
        ],
        compiler_params=pltpu.CompilerParams(
            collective_id=0, has_side_effects=True, vmem_limit_bytes=48 << 20
        ),
    )(target, facet, table, phase, heading, field, weights)


def body(
    field_in,
    heading_in,
    launch_domain,
    hop_domain,
    hit_facet,
    path_phase,
    facet_polar,
    facet_azimuth,
    facet_tilt,
    surface_resistance,
    surface_reactance,
    kernel,
):
    grid = (ROWS, LANES)
    target = jnp.concatenate(
        [launch_domain.reshape(1, *grid), hop_domain.reshape(BOUNCES - 1, *grid)], axis=0
    )
    facet = hit_facet.reshape(BOUNCES, *grid)
    phase = path_phase.reshape(BOUNCES, *grid)
    heading = heading_in.reshape(3, *grid)
    table = jnp.concatenate(
        [
            p.reshape(32, 256)
            for p in (
                facet_polar, facet_azimuth, facet_tilt, surface_resistance, surface_reactance
            )
        ],
        axis=0,
    )
    far, exit_field = main(target, facet, table, phase, heading, field_in, kernel)
    spot = (lax.axis_index("dom") % 8) * BINS + lax.axis_index("bin")
    return lax.dynamic_slice_in_dim(far, spot * 4, 4, axis=1), exit_field


def solution(mesh):
    both = ("dom", "bin")
    in_specs = (
        P(None, both),
        P(None, both),
        P(both, None),
        P(None, both, None),
        P(None, both),
        P(None, both),
        P("dom"),
        P("dom"),
        P("dom"),
        P("dom"),
        P("dom"),
        P(None, both, None),
    )
    out_specs = (P(None, both), P(None, both))
    return jax.shard_map(body, mesh=mesh, in_specs=in_specs, out_specs=out_specs, check_vma=False)
```

time: 1020 us -> 95.3 us (0.09); the launches traced: 1010 us -> 94.6 us
  local copies, waits for them, and re-layouts: 497 us -> 8.7 us
  other arithmetic: 217 us -> 0.81 us
  starting transfers between devices: 126 us -> 0 us
  Pallas kernels: 0 us -> 84.4 us
  waiting for transfers between devices: 82.4 us -> 0 us
  blocking collectives: 76.3 us -> 0 us
    scatter x12 -> x0, local copies, waits for them, and re-layouts: 237 us -> none  [the longest x4 121 us: body(): send_heading = jnp.zeros((3, domains * capacity), jnp.float32).at[:, slot...]
    scatter-add x4 -> x0, other arithmetic: 198 us -> none  [body(): facet_sums = facet_sums.at[:, got_ids].add(out_field)]
    gather x15 -> x0, local copies, waits for them, and re-layouts: 185 us -> none  [the longest x8 131 us: body(): facet_rows = jnp.take(frame_local, got_ids, axis=1)]
    all_to_all x13 -> x0, starting transfers between devices: 126 us -> none  [the longest x8 88.8 us: sent_together(): lax.all_to_all(both, axis, split_axis=split_dim, concat_axis=concat_dim,...]
    pallas_call x0 -> x1, Pallas kernels: none -> 84.4 us  [main(): pl.pallas_call(main_kernel, out_shape=(jax.ShapeDtypeStruct((8, LANES), F...]
    all_to_all x13 -> x0, waiting for transfers between devices: 82.4 us -> none  [the longest x8 50.7 us: sent_together(): lax.all_to_all(both, axis, split_axis=split_dim, concat_axis=concat_dim,...]
    unnamed x1 -> x0, blocking collectives: 76.3 us -> none
    reshape x9 -> x5, local copies, waits for them, and re-layouts: 26 us -> 3.85 us  [body(): p.reshape(32, 256)]
  transfers between devices with their start and end apart: 13 -> 0, of which waited for: 7 -> 0; matrix products, arithmetic and copies ran while one was open for 39% -> 0% of each run, Pallas kernels for 0% -> 0%
where the time goes in v1:
time: 95.3 us; the launch traced here: 94.6 us
  Pallas kernels  84.4 us (89%)
  local copies, waits for them, and re-layouts  8.7 us (9%)
    pallas_call x1, Pallas kernels, main(): pl.pallas_call(main_kernel, out_shape=(jax.ShapeDtypeStruct((8, LANES), F...  84.4 us
    unnamed x11, local copies, waits for them, and re-layouts  4.77 us
    reshape x5, local copies, waits for them, and re-layouts, body(): p.reshape(32, 256)  3.85 us

profile of v1, /device:TPU:1, one launch (start us, length us, event | category | flops | bytes accessed | tf_op | source)
XLA Modules:
  0.0 94.6 jit_solution(15757449553110242048)
XLA Ops:
  0.6 0.8 pad_add_fusion.target
  1.4 0.8 copy.22
  2.3 0.8 reshape.37
  3.1 0.8 reshape.38
  3.9 0.8 reshape.39
  4.6 0.8 reshape.40
  5.4 0.8 reshape.41
  6.2 0.8 copy.21
  7.1 0.8 copy.23
  7.9 0.0 copy-start
  7.9 0.9 copy-done
  8.8 84.4 %shard_map.131 = (f32[8,128]{1,0:T(8,128)S(1)}, f32[8,4096]{1,0:T(8,128)S(1)}) custom-call(s32[4,32,128]{2,1,0:T(8,128)S(1)} %pad_add_fusion.target, s32[4,32,128]{2,1,0:T(8,128)S(1)} %bitcast.14, f32[160,256]{1,0:T(8,128)S(1)} %constant_dynamic-update-slice_fusion.table, f32[4,32,128]{2,1,0:T(8,128)S(1)} %bitcast.15, f32[3,32,128]{2,1,0:T(8,128)S(1)} %bitcast.16, ...), custom_call_target="tpu_custom_call" | custom-call | tf_op jit(solution)/shard_map/pallas_call | solution.py:398
  93.2 0.1 constant_dynamic-slice_fusion
  93.3 0.7 copy.14
  94.0 0.7 copy.29
  (5 shorter events, 0.0 us)
Async XLA Ops:
  7.9 0.9 copy-start

commit v2 on v1

--- a/solution.py
+++ b/solution.py
@@ -123,7 +123,7 @@
             mine = place[:, LANES * w : LANES * (w + 1)]
             slots[b, n : n + 1, :] = doms[n] * CAP + mine
             places.append(mine)
-        ids = jnp.concatenate([facet[b, 2 * j + w : 2 * j + w + 1, :] for w in range(2)], axis=1)
+        ids = facet[pl.ds(b, 1), block * j : block * (j + 1)]
         left.append(
             jnp.concatenate(
                 [
@@ -136,7 +136,8 @@
     packed = lax.dot_general(
         jnp.concatenate(left, axis=1), one_hot(places, CAP), LAST, preferred_element_type=F32
     ).astype(I32)
-    ids_out[:, b, :] = packed[:DOMS] * 128 + packed[DOMS:]
+    row = packed[:DOMS]
+    ids_out[:, b, :] = (row & 31) * 256 + (row >> 5) * 128 + packed[DOMS:]
 
 
 def reflection(b, frame, phase, heading, coef):
@@ -179,23 +180,27 @@
 
 
 def main_kernel(
-    target, facet, table, phase, heading_in, field_in, weights,
+    launch_hbm, hops_hbm, facet_hbm, phase_hbm, heading_hbm, field_hbm,
+    polar_hbm, azimuth_hbm, tilt_hbm, res_hbm, rea_hbm, weights,
     far, exit_field,
-    held, weight_sem,
+    held, target, facet, phase_in, heading_in, field_in, params,
     ids_send, ids_got, slots, rows_table,
-    facts_send, facts_got, frame, heading, coef, field,
+    facts_send, facts_got, frame, phase, heading, coef, field,
     fields_send, fields_got, sums, sums_got, partial, along_got, piece, last_got,
-    ids_sems, facts_ssem, facts_rsem, fields_ssem, fields_rsem, sums_sems, along_sems, last_sems,
+    fetch_sems, ids_ssem, ids_rsem, facts_ssem, facts_rsem, fields_ssem, fields_rsem,
+    sums_sems, along_sems, last_sems,
 ):
     me, my_bin = lax.axis_index("dom"), lax.axis_index("bin")
     z, y, core = me // 8, (me // 2) % 4, me % 2
 
-    def partner(k):
-        return ((z + k // 8) % 8) * 8 + ((y + (k // 2) % 4) % 4) * 2 + (core + k % 2) % 2
+    def partner(kz, q):
+        return ((z + kz) % 8) * 8 + ((y + q // 2) % 4) * 2 + (core + q % 2) % 2
 
     def same_z(k):
-        dom = z * 8 + ((y + (k // 2) % 4) % 4) * 2 + (core + k % 2) % 2
-        return dom, (my_bin + k // 8) % BINS
+        return partner(0, k % 8), (my_bin + k // 8) % BINS
+
+    def near_first(i):
+        return (8 + ((i + 1) // 2) * (2 * (i % 2) - 1)) % 8
 
     def send(source, landing, ssem, rsem, dom, bin_at):
         pltpu.make_async_remote_copy(
@@ -206,60 +211,103 @@
     def await_bytes(ref, sem):
         pltpu.make_async_copy(ref, ref, sem).wait()
 
-    fetch = pltpu.make_async_copy(weights, held, weight_sem)
-    fetch.start()
+    moves = [
+        (launch_hbm, target.at[pl.ds(0, 1)]),
+        (hops_hbm, target.at[pl.ds(1, BOUNCES - 1)]),
+        (facet_hbm, facet),
+        (polar_hbm, params.at[0]),
+        (azimuth_hbm, params.at[1]),
+        (tilt_hbm, params.at[2]),
+        (res_hbm, params.at[3]),
+        (rea_hbm, params.at[4]),
+        (heading_hbm, heading_in),
+        (phase_hbm, phase_in),
+        (field_hbm, field_in),
+        (weights, held),
+    ]
+    fetches = [
+        pltpu.make_async_copy(source, landing, fetch_sems.at[i])
+        for i, (source, landing) in enumerate(moves)
+    ]
+    for fetch in fetches:
+        fetch.start()
     barrier = pltpu.get_barrier_semaphore()
 
     @pl.loop(1, DOMS)
     def _(k):
-        pl.semaphore_signal(barrier, inc=1, device_id=(partner(k), my_bin), device_id_type=MESH)
+        dom = partner(k // 8, k % 8)
+        pl.semaphore_signal(barrier, inc=1, device_id=(dom, my_bin), device_id_type=MESH)
 
     @pl.loop(8, 32)
     def _(k):
         pl.semaphore_signal(barrier, inc=1, device_id=same_z(k), device_id_type=MESH)
 
+    for fetch in fetches[:3]:
+        fetch.wait()
+
     @pl.loop(0, BOUNCES)
     def _(b):
         ranks(b, target, facet, ids_send, slots)
 
-    for k in range(3):
-        heading[k] = heading_in[k]
+    pl.semaphore_wait(barrier, DOMS - 1 + 24)
+
+    @pl.loop(0, DOMS)
+    def _(k):
+        kz = near_first(k // 8)
+        dom = partner(kz, k % 8)
+
+        @pl.when(k > 0)
+        def _():
+            send(ids_send.at[dom], ids_got.at[me], ids_ssem, ids_rsem.at[kz], dom, my_bin)
+
+    ids_got[me] = ids_send[me]
+
+    for fetch in fetches[3:11]:
+        fetch.wait()
+    for p in range(PARAMS):
+        rows = jnp.concatenate([params[p, 0:32, :], params[p, 32:64, :]], axis=1)
+        big, small = split(rows)
+        rows_table[32 * p : 32 * (p + 1)] = big
+        rows_table[32 * (PARAMS + p) : 32 * (PARAMS + p + 1)] = small
     for n in range(ROWS):
-        field[n] = field_in[:, n * LANES : (n + 1) * LANES]
-    big, small = split(table[...])
-    rows_table[: 32 * PARAMS] = big
-    rows_table[32 * PARAMS :] = small
-
-    pl.semaphore_wait(barrier, DOMS - 1 + 24)
-
-    @pl.loop(1, DOMS)
-    def _(k):
-        dom = partner(k)
-        send(ids_send.at[dom], ids_got.at[me], ids_sems.at[0], ids_sems.at[1], dom, my_bin)
-
-    ids_got[me] = ids_send[me]
-    await_bytes(ids_send.at[pl.ds(0, DOMS - 1)], ids_sems.at[1])
-
-    senders = BATCH // EACH
+        lanes = slice(n * LANES, (n + 1) * LANES)
+        heading[:, n, :] = heading_in[:, lanes]
+        phase[:, n, :] = phase_in[:, lanes]
+        field[n] = field_in[:, lanes]
 
     @pl.loop(0, HALVES)
     def _(h):
-        @pl.loop(0, DOMS // senders)
-        def _(g):
-            doms = [partner(g * senders + i) for i in range(senders)]
-            asked = [ids_got[dom, pl.ds(EACH * h + w, 1), :] for dom in doms for w in range(EACH)]
-
-            def store(i, p, value):
-                facts_send[h, doms[i // EACH], p, i % EACH : i % EACH + 1, :] = value
+        @pl.loop(0, 8)
+        def _(i):
+            kz = near_first(i)
+            first = ((z + 8 - kz) % 8) * 8
+
+            @pl.when((h == 0) & (i == 0))
+            def _():
+                await_bytes(ids_send.at[pl.ds(0, 7)], ids_rsem.at[0])
+
+            @pl.when((h == 0) & (i > 0))
+            def _():
+                await_bytes(ids_send.at[pl.ds(0, 8)], ids_rsem.at[kz])
+
+            asked = [
+                ids_got[first + q, pl.ds(EACH * h + w, 1), :] for q in range(8) for w in range(EACH)
+            ]
+
+            def store(n, p, value):
+                facts_send[h, first + n // EACH, p, n % EACH : n % EACH + 1, :] = value
 
             lookup(rows_table, asked, store)
-            for i in range(senders):
-
-                @pl.when(g * senders + i > 0)
+
+            @pl.loop(0, 8)
+            def _(q):
+                dom = partner(8 - kz, q)
+
+                @pl.when((i > 0) | (q > 0))
                 def _():
                     send(
-                        facts_send.at[h, doms[i]], facts_got.at[h, me],
-                        facts_ssem.at[h], facts_rsem.at[h], doms[i], my_bin,
+                        facts_send.at[h, dom], facts_got.at[h, me],
+                        facts_ssem.at[h], facts_rsem.at[h], dom, my_bin,
                     )
 
         facts_got[h, me] = facts_send[h, me]
@@ -301,13 +349,18 @@
             fields_send[2 * hi, b] = total[8 * hi : 8 * hi + 8, :LANES]
             fields_send[2 * hi + 1, b] = total[8 * hi : 8 * hi + 8, LANES:]
 
-        @pl.loop(1, DOMS)
+        @pl.loop(0, DOMS)
         def _(k):
-            dom = partner(k)
-            send(
-                fields_send.at[dom, b], fields_got.at[b, me],
-                fields_ssem.at[b], fields_rsem.at[b], dom, my_bin,
-            )
+            pair = k // 16
+            kz = (1 - (k // 8) % 2) * (4 + pair) + ((k // 8) % 2) * (3 - pair)
+            dom = partner(kz, k % 8)
+
+            @pl.when((kz > 0) | (k % 8 > 0))
+            def _():
+                send(
+                    fields_send.at[dom, b], fields_got.at[b, me],
+                    fields_ssem.at[b], fields_rsem.at[b, pair], dom, my_bin,
+                )
 
         fields_got[b, me] = fields_send[me, b]
 
@@ -318,21 +371,34 @@
 
     @pl.loop(0, BOUNCES)
     def _(b):
-        await_bytes(fields_got.at[b, pl.ds(0, DOMS - 1)], fields_rsem.at[b])
-
-        @pl.loop(0, DOMS // BATCH)
-        def _(g):
-            rows = [ids_got[g * BATCH + i, pl.ds(b, 1), :] for i in range(BATCH)]
-            sums[...] += gathered_sums(rows, [fields_got[b, g * BATCH + i] for i in range(BATCH)])
+        @pl.loop(0, 4)
+        def _(pair):
+            @pl.when(pair < 3)
+            def _():
+                await_bytes(fields_got.at[b, pl.ds(0, 16)], fields_rsem.at[b, pair])
+
+            @pl.when(pair == 3)
+            def _():
+                await_bytes(fields_got.at[b, pl.ds(0, 15)], fields_rsem.at[b, 3])
+
+            firsts = [((z + 8 - kz) % 8) * 8 for kz in (4 + pair, 3 - pair)]
+            senders = [first + q for first in firsts for q in range(8)]
+            total = gathered_sums(
+                [ids_got[dom, pl.ds(b, 1), :] for dom in senders],
+                [fields_got[b, dom] for dom in senders],
+            )
+            for j in range(2):
+                sums[j] += total[:, LANES * j : LANES * (j + 1)]
 
     for k in range(1, BINS):
         other = (my_bin + k) % BINS
         send(
-            sums.at[pl.ds(pl.multiple_of(other * 64, 64), 64)], sums_got.at[k - 1],
+            sums.at[other // 2, pl.ds(pl.multiple_of((other % 2) * 128, 128), 128)],
+            sums_got.at[k - 1],
             sums_sems.at[0, k - 1], sums_sems.at[1, k - 1], me, other,
         )
-    mine = sums[pl.ds(pl.multiple_of(my_bin * 64, 64), 64), :]
-    fetch.wait()
+    mine = sums[my_bin // 2, pl.ds(pl.multiple_of((my_bin % 2) * 128, 128), 128), :]
+    fetches[11].wait()
     for k in range(1, BINS):
         await_bytes(sums_got.at[k - 1], sums_sems.at[1, k - 1])
         mine = mine + sums_got[k - 1]
@@ -343,7 +409,9 @@
     for at in range(0, 1024, width):
         real, imag = jnp.zeros((8, width), F32), jnp.zeros((8, width), F32)
         for hi in range(8):
-            left = mine[8 * hi : 8 * hi + 8]
+            left = jnp.concatenate(
+                [mine[16 * hi : 16 * hi + 8], mine[16 * hi + 8 : 16 * hi + 16]], axis=1
+            )
             lines = slice(256 * hi, 256 * (hi + 1))
             real = real + jnp.dot(left, held[0, lines, at : at + width], preferred_element_type=F32)
             imag = imag + jnp.dot(left, held[1, lines, at : at + width], preferred_element_type=F32)
@@ -380,7 +448,7 @@
         tile = tile + last_got[k]
     far[...] = tile
 
-    await_bytes(ids_send.at[pl.ds(0, DOMS - 1)], ids_sems.at[0])
+    await_bytes(ids_send.at[pl.ds(0, DOMS - 1)], ids_ssem)
     for h in range(HALVES):
         await_bytes(facts_send.at[h, pl.ds(0, DOMS - 1)], facts_ssem.at[h])
     for b in range(BOUNCES):
@@ -391,7 +459,7 @@
     await_bytes(last_got.at[pl.ds(0, 31)], last_sems.at[0])
 
 
-def main(target, facet, table, phase, heading, field, weights):
+def main(*args):
     vmem = pltpu.VMEM
     dma = pltpu.SemaphoreType.DMA
     whole = pl.BlockSpec(memory_space=pltpu.VMEM)
@@ -401,11 +469,16 @@
             jax.ShapeDtypeStruct((8, LANES), F32),
             jax.ShapeDtypeStruct((8, ROWS * LANES), F32),
         ),
-        in_specs=[whole] * 6 + [pl.BlockSpec(memory_space=pl.ANY)],
+        in_specs=[pl.BlockSpec(memory_space=pltpu.HBM)] * 12,
         out_specs=(whole, whole),
         scratch_shapes=[
             vmem((2, 2048, 1024), BF16),
-            dma,
+            vmem((BOUNCES, ROWS, LANES), I32),
+            vmem((BOUNCES, ROWS * LANES), I32),
+            vmem((BOUNCES, ROWS * LANES), F32),
+            vmem((3, ROWS * LANES), F32),
+            vmem((8, ROWS * LANES), F32),
+            vmem((PARAMS, 64, LANES), F32),
             vmem((DOMS, BOUNCES, CAP), I32),
             vmem((DOMS, BOUNCES, CAP), I32),
             vmem((BOUNCES, ROWS, LANES), I32),
@@ -413,30 +486,33 @@
             vmem((HALVES, DOMS, PARAMS, EACH, CAP), F32),
             vmem((HALVES, DOMS, PARAMS, EACH, CAP), F32),
             vmem((PARAMS, ROWS, LANES), F32),
+            vmem((BOUNCES, ROWS, LANES), F32),
             vmem((3, ROWS, LANES), F32),
             vmem((6, ROWS, LANES), F32),
             vmem((ROWS, 8, LANES), F32),
             vmem((DOMS, BOUNCES, 8, CAP), F32),
             vmem((BOUNCES, DOMS, 8, CAP), F32),
-            vmem((256, 256), F32),
-            vmem((BINS - 1, 64, 256), F32),
+            vmem((2, 256, LANES), F32),
+            vmem((BINS - 1, 128, LANES), F32),
             vmem((8, 8, LANES), F32),
             vmem((8, 8, LANES), F32),
             vmem((8, LANES), F32),
             vmem((32, 8, LANES), F32),
-            dma((2,)),
+            dma((12,)),
+            dma,
+            dma((8,)),
             dma((HALVES,)),
             dma((HALVES,)),
             dma((BOUNCES,)),
-            dma((BOUNCES,)),
+            dma((BOUNCES, 4)),
             dma((2, BINS - 1)),
             dma((2,)),
             dma((2,)),
         ],
         compiler_params=pltpu.CompilerParams(
-            collective_id=0, has_side_effects=True, vmem_limit_bytes=48 << 20
+            collective_id=0, has_side_effects=True, vmem_limit_bytes=67043328
         ),
-    )(target, facet, table, phase, heading, field, weights)
+    )(*args)
 
 
 def body(
@@ -454,23 +530,19 @@
     kernel,
 ):
     grid = (ROWS, LANES)
-    target = jnp.concatenate(
-        [launch_domain.reshape(1, *grid), hop_domain.reshape(BOUNCES - 1, *grid)], axis=0
+    params = (facet_polar, facet_azimuth, facet_tilt, surface_resistance, surface_reactance)
+    far, exit_field = main(
+        launch_domain.reshape(1, *grid),
+        hop_domain.reshape(BOUNCES - 1, *grid),
+        hit_facet,
+        path_phase,
+        heading_in,
+        field_in,
+        *(p.reshape(64, LANES) for p in params),
+        kernel,
     )
-    facet = hit_facet.reshape(BOUNCES, *grid)
-    phase = path_phase.reshape(BOUNCES, *grid)
-    heading = heading_in.reshape(3, *grid)
-    table = jnp.concatenate(
-        [
-            p.reshape(32, 256)
-            for p in (
-                facet_polar, facet_azimuth, facet_tilt, surface_resistance, surface_reactance
-            )
-        ],
-        axis=0,
-    )
-    far, exit_field = main(target, facet, table, phase, heading, field_in, kernel)
-    spot = (lax.axis_index("dom") % 8) * BINS + lax.axis_index("bin")
+    dom, bin_at = lax.axis_index("dom"), lax.axis_index("bin")
+    spot = (dom % 8) * BINS + bin_at
     return lax.dynamic_slice_in_dim(far, spot * 4, 4, axis=1), exit_field
 
 

time: 95.3 us -> 85.9 us (0.901)
  local copies, waits for them, and re-layouts: 8.7 us -> 2.98 us
  Pallas kernels: 84.4 us -> 82.1 us
    reshape x5 -> x0, local copies, waits for them, and re-layouts: 3.85 us -> none  [body(): p.reshape(32, 256)]
    unnamed x11 -> x2, local copies, waits for them, and re-layouts: 4.77 us -> 2.22 us
    pallas_call x1, Pallas kernels: 84.4 us -> 82.1 us  [main(): pl.pallas_call(main_kernel, out_shape=(jax.ShapeDtypeStruct((8, LANES), F...]
where the time goes in v2:
time: 85.9 us; the launch traced here: 85.8 us
  Pallas kernels  82.1 us (96%)
  local copies, waits for them, and re-layouts  2.98 us (3%)
    pallas_call x1, Pallas kernels, main(): pl.pallas_call(main_kernel, out_shape=(jax.ShapeDtypeStruct((8, LANES), F...  82.1 us
    unnamed x2, local copies, waits for them, and re-layouts  2.22 us

profile of v2, /device:TPU:1, one launch (start us, length us, event | category | flops | bytes accessed | tf_op | source)
XLA Modules:
  0.0 85.8 jit_solution(17350108381225424674)
XLA Ops:
  0.7 82.1 %shard_map.131 = (f32[8,128]{1,0:T(8,128)}, f32[8,4096]{1,0:T(8,128)}) custom-call(s32[1,32,128]{2,1,0:T(8,128)} %bitcast.13, s32[3,32,128]{2,1,0:T(8,128)} %bitcast.7, s32[4,4096]{1,0:T(4,128)} %facet_hbm.1, f32[4,4096]{1,0:T(4,128)} %phase_hbm.1, f32[3,4096]{1,0:T(4,128)} %heading_hbm.1, f32[8,4096]{1,0:T(8,128)} %field_hbm.1, f32[64,128]{1,0:T(8,128)} %bitcast.8, ...), custom_call_target="tpu_custom_call" | custom-call | tf_op jit(solution)/shard_map/pallas_call | solution.py:466
  82.8 0.8 constant_dynamic-slice_fusion
  83.5 0.7 copy.14
  84.2 1.6 %copy.16 = f32[8,4096]{1,0:T(8,128)} copy(f32[8,4096]{1,0:T(8,128)} %get-tuple-element.11) | data formatting | bytes 262144

commit v3 on v2

--- a/solution.py
+++ b/solution.py
@@ -510,9 +510,9 @@
             dma((2,)),
         ],
         compiler_params=pltpu.CompilerParams(
-            collective_id=0, has_side_effects=True, vmem_limit_bytes=67043328
+            collective_id=0, has_side_effects=True, vmem_limit_bytes=48 << 20
         ),
-    )(*args)
+    )(*(pltpu.with_memory_space_constraint(a, pltpu.HBM) for a in args))
 
 
 def body(

time: 85.9 us -> 83.8 us (0.976)
  local copies, waits for them, and re-layouts: 2.98 us -> 1.39 us
    unnamed x2, local copies, waits for them, and re-layouts: 2.22 us -> 1.31 us
where the time goes in v3:
time: 83.8 us; the launch traced here: 83.7 us
  Pallas kernels  81.7 us (97%)
  local copies, waits for them, and re-layouts  1.39 us (2%)
    pallas_call x1, Pallas kernels, main(): pl.pallas_call(main_kernel, out_shape=(jax.ShapeDtypeStruct((8, LANES), F...  81.7 us

profile of v3, /device:TPU:1, one launch (start us, length us, event | category | flops | bytes accessed | tf_op | source)
XLA Modules:
  0.0 83.7 jit_solution(8482167826501787169)
XLA Ops:
  0.7 81.7 %shard_map.131 = (f32[8,128]{1,0:T(8,128)S(1)}, f32[8,4096]{1,0:T(8,128)S(1)}) custom-call(s32[1,32,128]{2,1,0:T(8,128)} %bitcast.13, s32[3,32,128]{2,1,0:T(8,128)} %bitcast.7, s32[4,4096]{1,0:T(4,128)} %facet_hbm.1, f32[4,4096]{1,0:T(4,128)} %phase_hbm.1, f32[3,4096]{1,0:T(4,128)} %heading_hbm.1, f32[8,4096]{1,0:T(8,128)} %field_hbm.1, f32[64,128]{1,0:T(8,128)} %bitcast.8, ...), custom_call_target="tpu_custom_call" | custom-call | tf_op jit(solution)/shard_map/pallas_call | solution.py:466
  82.3 0.1 constant_dynamic-slice_fusion
  82.4 0.7 copy.14
  83.1 0.7 copy.16

commit v4 on v3

--- a/solution.py
+++ b/solution.py
@@ -193,6 +193,15 @@
     me, my_bin = lax.axis_index("dom"), lax.axis_index("bin")
     z, y, core = me // 8, (me // 2) % 4, me % 2
 
+    places = [((y + q // 2) % 4) * 2 + (core + q % 2) % 2 for q in range(8)]
+
+    def each_of_plane(plane, skip_first, action):
+        for q in range(8):
+            if q == 0:
+                pl.when(jnp.logical_not(skip_first))(lambda: action(plane * 8 + places[0]))
+            else:
+                action(plane * 8 + places[q])
+
     def partner(kz, q):
         return ((z + kz) % 8) * 8 + ((y + q // 2) % 4) * 2 + (core + q % 2) % 2
 
@@ -233,10 +242,12 @@
         fetch.start()
     barrier = pltpu.get_barrier_semaphore()
 
-    @pl.loop(1, DOMS)
-    def _(k):
-        dom = partner(k // 8, k % 8)
-        pl.semaphore_signal(barrier, inc=1, device_id=(dom, my_bin), device_id_type=MESH)
+    @pl.loop(0, 8)
+    def _(kz):
+        def greet(dom):
+            pl.semaphore_signal(barrier, inc=1, device_id=(dom, my_bin), device_id_type=MESH)
+
+        each_of_plane((z + kz) % 8, kz == 0, greet)
 
     @pl.loop(8, 32)
     def _(k):
@@ -251,14 +262,14 @@
 
     pl.semaphore_wait(barrier, DOMS - 1 + 24)
 
-    @pl.loop(0, DOMS)
-    def _(k):
-        kz = near_first(k // 8)
-        dom = partner(kz, k % 8)
-
-        @pl.when(k > 0)
-        def _():
+    @pl.loop(0, 8)
+    def _(i):
+        kz = near_first(i)
+
+        def ask(dom):
             send(ids_send.at[dom], ids_got.at[me], ids_ssem, ids_rsem.at[kz], dom, my_bin)
+
+        each_of_plane((z + kz) % 8, i == 0, ask)
 
     ids_got[me] = ids_send[me]
 
@@ -299,16 +310,13 @@
 
             lookup(rows_table, asked, store)
 
-            @pl.loop(0, 8)
-            def _(q):
-                dom = partner(8 - kz, q)
-
-                @pl.when((i > 0) | (q > 0))
-                def _():
-                    send(
-                        facts_send.at[h, dom], facts_got.at[h, me],
-                        facts_ssem.at[h], facts_rsem.at[h], dom, my_bin,
-                    )
+            def answer(dom):
+                send(
+                    facts_send.at[h, dom], facts_got.at[h, me],
+                    facts_ssem.at[h], facts_rsem.at[h], dom, my_bin,
+                )
+
+            each_of_plane((z + 8 - kz) % 8, i == 0, answer)
 
         facts_got[h, me] = facts_send[h, me]
 
@@ -349,18 +357,18 @@
             fields_send[2 * hi, b] = total[8 * hi : 8 * hi + 8, :LANES]
             fields_send[2 * hi + 1, b] = total[8 * hi : 8 * hi + 8, LANES:]
 
-        @pl.loop(0, DOMS)
-        def _(k):
-            pair = k // 16
-            kz = (1 - (k // 8) % 2) * (4 + pair) + ((k // 8) % 2) * (3 - pair)
-            dom = partner(kz, k % 8)
-
-            @pl.when((kz > 0) | (k % 8 > 0))
-            def _():
+        @pl.loop(0, 8)
+        def _(i):
+            pair = i // 2
+            kz = (1 - i % 2) * (4 + pair) + (i % 2) * (3 - pair)
+
+            def give(dom):
                 send(
                     fields_send.at[dom, b], fields_got.at[b, me],
                     fields_ssem.at[b], fields_rsem.at[b, pair], dom, my_bin,
                 )
+
+            each_of_plane((z + kz) % 8, i == 7, give)
 
         fields_got[b, me] = fields_send[me, b]
 

time: 83.8 us -> 81.1 us (0.968)
  Pallas kernels: 81.7 us -> 79 us
    pallas_call x1, Pallas kernels: 81.7 us -> 79 us  [main(): pl.pallas_call(main_kernel, out_shape=(jax.ShapeDtypeStruct((8, LANES), F...]
where the time goes in v4:
time: 81.1 us
  Pallas kernels  79 us (97%)
  local copies, waits for them, and re-layouts  1.39 us (2%)
    pallas_call x1, Pallas kernels, main(): pl.pallas_call(main_kernel, out_shape=(jax.ShapeDtypeStruct((8, LANES), F...  79 us

profile of v4, /device:TPU:1, one launch (start us, length us, event | category | flops | bytes accessed | tf_op | source)
XLA Modules:
  0.0 81.1 jit_solution(3711513716897570522)
XLA Ops:
  0.7 79.0 %shard_map.131 = (f32[8,128]{1,0:T(8,128)S(1)}, f32[8,4096]{1,0:T(8,128)S(1)}) custom-call(s32[1,32,128]{2,1,0:T(8,128)} %bitcast.13, s32[3,32,128]{2,1,0:T(8,128)} %bitcast.7, s32[4,4096]{1,0:T(4,128)} %facet_hbm.1, f32[4,4096]{1,0:T(4,128)} %phase_hbm.1, f32[3,4096]{1,0:T(4,128)} %heading_hbm.1, f32[8,4096]{1,0:T(8,128)} %field_hbm.1, f32[64,128]{1,0:T(8,128)} %bitcast.8, ...), custom_call_target="tpu_custom_call" | custom-call | tf_op jit(solution)/shard_map/pallas_call | solution.py:474
  79.7 0.1 constant_dynamic-slice_fusion
  79.8 0.7 copy.14
  80.4 0.7 copy.16
